TPU v7x, 32 devices: a whole 2x2x4 slice. The times are simulated.
32 devices in a mesh: hist: 8 (over z, x), cand: 4 (over y, core).
Axes of the slice: x: 2, y: 2, z: 4, core: 2. Of those that a mesh axis runs over, the one named last changes fastest.
Arguments:
- cand_emb: bfloat16 [4, 256, 1024], P('cand', 'hist'), may hold values from -6 to 6
- cand_user: int32 [4, 256], P('cand'), may hold values from 0 to 3
- kv_cache: bfloat16 [4, 64, 2, 128, 1024], P('cand', 'hist'), may hold values from -6 to 6
- tile_user: int32 [4, 64], P('cand', 'hist'), may hold values from 0 to 3
- tile_len: int32 [4, 64], P('cand', 'hist'), may hold values from 1 to 128
- w_uq: bfloat16 [2048, 1024], P('cand'), may hold values from -0.1875 to 0.1875
- w_out: bfloat16 [1024, 1024], P('cand'), may hold values from -0.1875 to 0.1875
Outputs:
- scored: bfloat16 [4, 256, 1024], P('cand', 'hist')
All inputs are finite; a program needn't handle non-finite values.
Results may differ from a plain program's by a relative error of at most 0.0053.
Values may be sent and summed in bfloat16 or wider, within the bound.
A program may use at most 128 MiB of HBM per device.

v0:
```python
import jax
import jax.numpy as jnp
from jax import lax
from jax.sharding import PartitionSpec as P

HEADS = 8


def times_rows(left, slab):
    return lax.dot_general(left, slab, (((1,), (1,)), ((), ())), preferred_element_type=jnp.float32)


def per_device(cand_emb, cand_user, kv_cache, tile_user, tile_len, w_uq, w_out):
    embeds = cand_emb[0]
    count = embeds.shape[0]
    width = embeds.shape[1]
    head_size = width // HEADS
    score_scale = 1.0 / head_size**0.5
    uq_full = times_rows(embeds, lax.all_gather(w_uq, "cand", axis=0, tiled=True))
    uq_full = jax.nn.silu(uq_full).astype(jnp.bfloat16)
    u_part = uq_full[:, :width]
    queries = uq_full[:, width:]
    all_queries = lax.all_gather(queries, "hist", axis=0, tiled=True)
    group_users = cand_user[0]
    caches = kv_cache[0]
    owners = tile_user[0]
    lengths = tile_len[0]
    tiles_here = caches.shape[0]
    tile_rows = caches.shape[2]
    row_ids = jnp.arange(tile_rows, dtype=jnp.int32)
    block_q = all_queries.reshape(lax.axis_size("hist") * count, HEADS, head_size)
    total = jnp.zeros((lax.axis_size("hist") * count, HEADS, head_size), jnp.float32)
    for tile in range(tiles_here):
        keys = caches[tile, 0].reshape(tile_rows, HEADS, head_size)
        values = caches[tile, 1].reshape(tile_rows, HEADS, head_size)
        allowed = (group_users[:, None] == owners[tile]) & (row_ids[None, :] < lengths[tile])
        scores = (
            jnp.einsum("qhd,khd->hqk", block_q, keys, preferred_element_type=jnp.float32)
            * score_scale
        )
        weights = jnp.where(allowed[None], jax.nn.silu(scores), 0.0).astype(jnp.bfloat16)
        total = total + jnp.einsum(
            "hqk,khd->qhd", weights, values, preferred_element_type=jnp.float32
        )
    attn = lax.psum_scatter(
        total.reshape(lax.axis_size("hist") * count, width), "hist", scatter_dimension=0, tiled=True
    )
    center = jnp.mean(attn, axis=1, keepdims=True)
    spread = jnp.mean((attn - center) ** 2, axis=1, keepdims=True)
    normed = (attn - center) / jnp.sqrt(spread + 1e-05)
    y_rows = (normed * u_part.astype(jnp.float32)).astype(jnp.bfloat16)
    projected = times_rows(y_rows, lax.all_gather(w_out, "cand", axis=0, tiled=True))
    result = (embeds.astype(jnp.float32) + projected).astype(jnp.bfloat16)
    return result[None]


def solution(mesh):
    in_specs = (
        P("cand", "hist", None),
        P("cand", None),
        P("cand", "hist", None, None, None),
        P("cand", "hist"),
        P("cand", "hist"),
        P("cand", None),
        P("cand", None),
    )
    out_specs = P("cand", "hist", None)
    return jax.shard_map(
        per_device, mesh=mesh, in_specs=in_specs, out_specs=out_specs, check_vma=False
    )
```

profile of v0, /device:TPU:0, one launch (start us, length us, event | category | flops | bytes accessed | tf_op | source)
XLA Modules:
  0.0 199.5 jit_solution(9853936113189179470)
XLA Ops:
  6.5 0.7 all-gather.3.cloned.1.call-update
  7.3 6.5 %copy.25 = bf16[1,8,2,128,1024]{3,4,2,1,0:T(8,128)(2,1)} copy(bf16[1,8,2,128,1024]{4,3,2,1,0:T(8,128)(2,1)} %param.9) | data formatting | bytes 8388608 | tf_op args[2]
  13.8 0.7 fusion.99
  15.0 0.7 iota_compare_fusion.7
  15.7 0.6 iota_compare_fusion.4
  16.3 0.6 iota_compare_fusion.5
  17.5 0.6 iota_compare_fusion.3
  18.1 0.7 iota_compare_fusion
  18.8 0.6 iota_compare_fusion.1
  19.5 0.7 fusion.100
  20.1 4.9 %compare_reduce_fusion = (pred[256]{0:T(512)(128)(4,1)S(1)}, pred[256]{0:T(512)(128)(4,1)S(1)}, pred[256]{0:T(512)(128)(4,1)S(1)}, pred[256]{0:T(512)(128)(4,1)S...) fusion(s32[1,256]{1,0:T(1,128)S(1)} %copy-done.3, ...), kind=kLoop, calls=%fused_computation.91 | loop fusion | flops 2048 | bytes 3104 | tf_op jit(solution)/shard_map/eq | solution.py:36
  25.0 0.7 broadcast_and_fusion.6
  25.8 0.7 broadcast_and_fusion.4
  26.8 3.5 %fusion.98 = (bf16[1,1,128,1024]{2,3,1,0:T(8,128)(2,1)S(1)}, bf16[1,1,128,1024]{2,3,1,0:T(8,128)(2,1)S(1)}, bf16[1,1,128,1024]{2,3,1,0:T(8,128)(2,1)S(1)}, bf16[...) fusion(bf16[8,2,128,1024]{2,3,1,0:T(8,128)(2,1)} %bitcast.120), kind=kLoop, calls=%fused_computation.133 | loop fusion | bytes 8388608 | tf_op jit(solution)/shard_map/slice | solution.py:34
  30.3 15.8 %all-gather.3.cloned.1.call-done = bf16[2048,1024]{1,0:T(8,128)(2,1)} async-done(((bf16[512,1024]{1,0:T(8,128)(2,1)}), bf16[2048,1024]{1,0:T(8,128)(2,1)}) %all-gather.3.cloned.1.call-update) | async-done | bytes 4194320 | tf_op jit(solution)/shard_map/all_gather | solution.py:19
  46.1 3.5 %multiply_convert_fusion = bf16[32,2048]{1,0:T(8,128)(2,1)S(1)} fusion(bf16[2048,1024]{1,0:T(8,128)(2,1)} %all-gather.3.cloned.1.call-done, bf16[1,32,1024]{2,1,0:T(8,128)(2,1)S(1)} %copy-done), kind=kOutput, calls=%fused_computation.67 | convolution fusion | flops 134545408 | bytes 4390912 | tf_op jit(solution)/shard_map/dot_general | solution.py:10
  49.7 31.4 %all_gather.10 = bf16[256,1024]{1,0:T(8,128)(2,1)S(1)} all-gather(bf16[32,1024]{1,0:T(8,128)(2,1)S(1)} %slice.152), channel_id=1, replica_groups=mesh['hist'=8,'cand'=4] {'hist'}, dimensions={0}, use_global_device_ids=true | all-gather | bytes 589824 | tf_op jit(solution)/shard_map/all_gather | solution.py:23
  81.1 2.7 %fusion.2 = f32[8,256,128]{1,2,0:T(8,128)} fusion(bf16[128,8,128]{0,2,1:T(8,128)(2,1)} %bitcast.136, bf16[128,8,128]{0,2,1:T(8,128)(2,1)} %bitcast.137, pred[256,128]{1,0:T(8,128)(4,1)} %get-tuple-element.52, bf16[256,1024]{1,0:T(8,128)(2,1)S(1)} %all_gather.10), kind=kOutput, calls=%fused_computation.26 | convolution fusion | flops 136052736 | bytes 2129920 | tf_op jit(solution)/shard_map/hqk,khd->qhd/dot_general | solution.py:42
  83.8 3.0 %convolution_add_fusion.6 = f32[8,256,128]{1,2,0:T(8,128)} fusion(f32[8,256,128]{1,2,0:T(8,128)} %fusion.2, bf16[128,8,128]{0,2,1:T(8,128)(2,1)} %bitcast.134, bf16[128,8,128]{0,2,1:T(8,128)(2,1)} %bitcast.135, pred[256,128]{1,0:T(8,128)(4,1)S(1)} %get-tuple-element.51, bf16[256,1024]{1,0:T(8,128)(2,1)S(1)} %all_gather.10), kind=kOutput, calls=%fused_computation.12 | convolution fusion | flops 136314880 | bytes 3178496 | tf_op jit(solution)/shard_map/hqk,khd->qhd/dot_general | solution.py:42
  86.9 3.1 %convolution_add_fusion.5 = f32[8,256,128]{1,2,0:T(8,128)} fusion(f32[8,256,128]{1,2,0:T(8,128)} %convolution_add_fusion.6, bf16[128,8,128]{0,2,1:T(8,128)(2,1)} %bitcast.132, bf16[128,8,128]{0,2,1:T(8,128)(2,1)} %bitcast.133, pred[256,128]{1,0:T(8,128)(4,1)} %get-tuple-element.50, bf16[256,1024]{1,0:T(8,128)(2,1)S(1)} %all_gather.10), kind=kOutput, calls=%fused_computation.10 | convolution fusion | flops 136314880 | bytes 3178496 | tf_op jit(solution)/shard_map/hqk,khd->qhd/dot_general | solution.py:42
  89.9 2.9 %convolution_add_fusion.4 = f32[8,256,128]{1,2,0:T(8,128)} fusion(f32[8,256,128]{1,2,0:T(8,128)} %convolution_add_fusion.5, bf16[128,8,128]{0,2,1:T(8,128)(2,1)S(1)} %bitcast.130, bf16[128,8,128]{0,2,1:T(8,128)(2,1)S(1)} %bitcast.131, pred[256,128]{1,0:T(8,128)(4,1)S(1)} %get-tuple-element.49, bf16[256,1024]{1,0:T(8,128)(2,1)S(1)} %all_gather.10), kind=kOutput, calls=%fused_computation.8 | convolution fusion | flops 136314880 | bytes 3178496 | tf_op jit(solution)/shard_map/hqk,khd->qhd/dot_general | solution.py:42
  92.8 2.9 %convolution_add_fusion.3 = f32[8,256,128]{1,2,0:T(8,128)} fusion(f32[8,256,128]{1,2,0:T(8,128)} %convolution_add_fusion.4, bf16[128,8,128]{0,2,1:T(8,128)(2,1)S(1)} %bitcast.128, bf16[128,8,128]{0,2,1:T(8,128)(2,1)S(1)} %bitcast.129, pred[256,128]{1,0:T(8,128)(4,1)S(1)} %get-tuple-element.48, bf16[256,1024]{1,0:T(8,128)(2,1)S(1)} %all_gather.10), kind=kOutput, calls=%fused_computation.6 | convolution fusion | flops 136314880 | bytes 3178496 | tf_op jit(solution)/shard_map/hqk,khd->qhd/dot_general | solution.py:42
  95.7 2.9 %convolution_add_fusion.2 = f32[8,256,128]{1,2,0:T(8,128)} fusion(f32[8,256,128]{1,2,0:T(8,128)} %convolution_add_fusion.3, bf16[128,8,128]{0,2,1:T(8,128)(2,1)S(1)} %bitcast.126, bf16[128,8,128]{0,2,1:T(8,128)(2,1)S(1)} %bitcast.127, pred[256,128]{1,0:T(8,128)(4,1)S(1)} %get-tuple-element.47, bf16[256,1024]{1,0:T(8,128)(2,1)S(1)} %all_gather.10), kind=kOutput, calls=%fused_computation.4 | convolution fusion | flops 136314880 | bytes 3178496 | tf_op jit(solution)/shard_map/hqk,khd->qhd/dot_general | solution.py:42
  98.6 1.9 convolution_add_fusion.1
  100.5 0.7 convolution_add_fusion
  101.2 1.3 copy.51
  102.6 0.7 all-gather.5.cloned.1.call-update
  103.2 63.6 %reduce-scatter.2.cloned.1.call-done = f32[32,1024]{1,0:T(8,128)} async-done(((f32[256,1024]{1,0:T(8,128)}), f32[32,1024]{1,0:T(8,128)}) %reduce-scatter.2.cloned.1.call-update) | async-done | bytes 131088 | tf_op jit(solution)/shard_map/reduce_scatter | solution.py:45
  166.8 1.0 reduce_sum.18
  167.9 1.1 multiply_reduce_fusion
  169.0 21.0 %all-gather.5.cloned.1.call-done = bf16[1024,1024]{1,0:T(8,128)(2,1)} async-done(((bf16[256,1024]{1,0:T(8,128)(2,1)}), bf16[1024,1024]{1,0:T(8,128)(2,1)}) %all-gather.5.cloned.1.call-update) | async-done | bytes 2097168 | tf_op jit(solution)/shard_map/all_gather | solution.py:52
  189.9 3.0 %fusion.1 = bf16[1,32,1024]{2,1,0:T(8,128)(2,1)} fusion(bf16[1024,1024]{1,0:T(8,128)(2,1)} %all-gather.5.cloned.1.call-done, f32[32,1024]{1,0:T(8,128)} %reduce-scatter.2.cloned.1.call-done, bf16[32,2048]{1,0:T(8,128)(2,1)S(1)} %multiply_convert_fusion, bf16[1,32,1024]{2,1,0:T(8,128)(2,1)S(1)} %copy-done, f32[32]{0:T(128)S(1)} %add_sqrt_fusion, ...), kind=kOutput, calls=%fused_computation.17 | convolution fusion | flops 67371008 | bytes 2425856 | tf_op jit(solution)/shard_map/dot_general | solution.py:10
  (19 shorter events, 1.5 us)
Async XLA Ops:
  6.5 39.6 %all-gather.3.cloned.1.call-start = ((), (), s32[]{:S(2)}) async-start(), calls=%async_computation.1 | async-start | bytes 5242880 | tf_op jit(solution)/shard_map/all_gather | solution.py:19
  7.3 6.5 %copy-start.1 = (s32[1,8]{1,0:T(1,128)S(1)}, s32[1,8]{1,0:T(1,128)}, u32[]{:S(2)}) copy-start(s32[1,8]{1,0:T(1,128)} %param.11) | copy-start | bytes 100
  7.3 12.2 %copy-start.2 = (s32[1,8]{1,0:T(1,128)S(1)}, s32[1,8]{1,0:T(1,128)}, u32[]{:S(2)}) copy-start(s32[1,8]{1,0:T(1,128)} %param.10) | copy-start | bytes 100
  7.3 12.9 %copy-start.3 = (s32[1,256]{1,0:T(1,128)S(1)}, s32[1,256]{1,0:T(1,128)}, u32[]{:S(2)}) copy-start(s32[1,256]{1,0:T(1,128)} %param.8) | copy-start | bytes 3076
  7.3 159.5 %reduce-scatter.2.cloned.1.call-start = ((), (), s32[]{:S(2)}) async-start(), calls=%async_computation.2 | async-start | bytes 1179648 | tf_op jit(solution)/shard_map/reduce_scatter | solution.py:45
  26.8 19.3 %copy-start = (bf16[1,32,1024]{2,1,0:T(8,128)(2,1)S(1)}, bf16[1,32,1024]{2,1,0:T(8,128)(2,1)}, u32[]{:S(2)}) copy-start(bf16[1,32,1024]{2,1,0:T(8,128)(2,1)} %param.7) | copy-start | bytes 196612
  102.5 87.4 %all-gather.5.cloned.1.call-start = ((), (), s32[]{:S(2)}) async-start(), calls=%async_computation.3 | async-start | bytes 2621440 | tf_op jit(solution)/shard_map/all_gather | solution.py:52
Sparse Core Ops, SparseCore 0:
  8.9 37.1 all-gather.2
  102.6 64.1 reduce-scatter.1
  168.4 21.4 all-gather.4
where the time goes:
time: 200 us
  waiting for transfers between devices  102 us (51%)
  blocking collectives  31.4 us (16%)
  matrix products  26.6 us (13%)
  other arithmetic  13.7 us (7%)
  between operations  13.3 us (7%)
  local copies, waits for them, and re-layouts  12.6 us (6%)
    reduce_scatter x1, waiting for transfers between devices, per_device(): lax.psum_scatter(total.reshape(lax.axis_size('hist') * count, width), 'hi...  63.6 us
    all_gather x1, blocking collectives, per_device(): all_queries = lax.all_gather(queries, 'hist', axis=0, tiled=True)  31.4 us
    all_gather x1, waiting for transfers between devices, per_device(): lax.all_gather(w_out, 'cand', axis=0, tiled=True)  21 us
    dot_general x8, matrix products, per_device(): jnp.einsum('hqk,khd->qhd', weights, values, preferred_element_type=jnp.fl...  20 us
    all_gather x1, waiting for transfers between devices, per_device(): lax.all_gather(w_uq, 'cand', axis=0, tiled=True)  15.8 us
    dot_general x2, matrix products, times_rows(): lax.dot_general(left, slab, (((1,), (1,)), ((), ())), preferred_element_t...  6.6 us
    unnamed x9, local copies, waits for them, and re-layouts  6.49 us
    lt x8, other arithmetic, per_device(): row_ids[None, :] < lengths[tile]  4.92 us
  transfers between devices with their start and end apart: 3, of which 3 were waited for; matrix products, arithmetic and copies ran while one was open for 13% of the time, Pallas kernels for 0%

commit v1 on v0

v1 whole, which is shorter than its diff:
```python
import functools

import jax
import jax.numpy as jnp
from jax import lax
from jax.experimental import pallas as pl
from jax.experimental.pallas import tpu as pltpu
from jax.sharding import PartitionSpec as P

HEADS = 8
BF16 = jnp.bfloat16
F32 = jnp.float32


def times_rows(left, slab):
    return lax.dot_general(left, slab, (((1,), (1,)), ((), ())), preferred_element_type=F32)


def half_silu(half):
    return half + half * jnp.tanh(half)


def loop(low, high, body):
    if high - low <= 8:
        for step in range(low, high):
            body(step)
    else:
        lax.fori_loop(low, high, lambda step, carry: (body(step), carry)[1], 0)


def kernel(
    nh, nc, emb_hbm, user_ref, kv_hbm, owner_ref, len_ref, wuq_hbm, wout_hbm, out_ref,
    emb, kv, wuq, wout, uq_send, uq_all, mask, part, landed,
    local_sem, emb_send, emb_recv, uq_ssem, uq_rsem, q_send, q_recv,
    part_send, part_recv, w_send, w_recv, wf_send, wf_recv,
):
    hist = lax.axis_index("hist")
    cand = lax.axis_index("cand")
    rows, width = emb.shape[1], emb.shape[2]
    feats = wuq.shape[0]
    slices = nc // 2
    head_size = width // HEADS
    tiles, tile_rows = kv.shape[0], kv.shape[2]
    chips = nc // 2
    mate = cand + 1 - 2 * lax.rem(cand, 2)

    def remote(src, dst, ssem, rsem, peer):
        return pltpu.make_async_remote_copy(
            src_ref=src, dst_ref=dst, send_sem=ssem, recv_sem=rsem,
            device_id=peer, device_id_type=pl.DeviceIdType.MESH,
        )

    def up_cand(step):
        return lax.rem(cand + step, nc)

    def down_cand(step):
        return lax.rem(cand + nc - step, nc)

    def up_hist(step):
        return lax.rem(hist + step, nh)

    def down_hist(step):
        return lax.rem(hist + nh - step, nh)

    load_emb = pltpu.make_async_copy(emb_hbm.at[0], emb.at[0], local_sem.at[0])
    load_wuq = pltpu.make_async_copy(wuq_hbm, wuq, local_sem.at[1])
    load_kv = pltpu.make_async_copy(kv_hbm.at[0], kv, local_sem.at[2])
    load_wout = pltpu.make_async_copy(wout_hbm, wout.at[cand], local_sem.at[3])
    load_emb.start()
    load_wuq.start()
    load_wout.start()
    load_kv.start()

    barrier = pltpu.get_barrier_semaphore()

    def greet_cand(step):
        pl.semaphore_signal(
            barrier, inc=1, device_id=(hist, up_cand(step)), device_id_type=pl.DeviceIdType.MESH
        )

    def greet_hist(step):
        pl.semaphore_signal(
            barrier, inc=1, device_id=(up_hist(step), cand), device_id_type=pl.DeviceIdType.MESH
        )

    loop(1, nc, greet_cand)
    loop(1, nh, greet_hist)
    pl.semaphore_wait(barrier, nc - 1 + nh - 1)

    def emb_copy(step):
        return remote(
            emb_hbm.at[0], emb.at[step], emb_send.at[step], emb_recv.at[step], (hist, up_cand(step))
        )

    loop(1, nc, lambda step: emb_copy(step).start())

    count = nh * rows
    users = jnp.broadcast_to(user_ref[...].astype(F32), (tile_rows, count)).T
    lane = lax.broadcasted_iota(jnp.int32, (count, tile_rows), 1)
    for tile in range(tiles):
        same = users == owner_ref[0, tile].astype(F32)
        valid = lane < len_ref[0, tile]
        mask[:, tile * tile_rows:(tile + 1) * tile_rows] = jnp.where(
            same & valid, 1.0, 0.0
        ).astype(BF16)

    load_wuq.wait()
    load_emb.wait()
    loop(1, nc, lambda step: emb_copy(step).wait())
    uq = times_rows(emb[...].reshape(nc * rows, width), wuq[...])
    uq = half_silu(uq * 0.5).astype(BF16).reshape(nc, rows, feats)
    uq_send[...] = uq
    uq_all[cand, hist] = uq[0]

    def uq_copy(step, slot):
        return remote(
            uq_send.at[step], uq_all.at[slot, hist], uq_ssem.at[step], uq_rsem.at[step],
            (hist, down_cand(step)),
        )

    loop(1, nc, lambda step: uq_copy(step, cand).start())

    def w_copy(step):
        return remote(
            wout_hbm, wout.at[cand], w_send.at[step], w_recv.at[step], (hist, up_cand(2 * step))
        )

    loop(1, chips, lambda step: w_copy(step).start())
    own_w = remote(wout_hbm, wout.at[cand], w_send.at[0], w_recv.at[0], (hist, mate))
    own_w.start()

    loop(1, nc, lambda step: uq_copy(step, up_cand(step)).wait())

    def q_copy(piece, step, slot):
        return remote(
            uq_all.at[slices + piece, slot], uq_all.at[slices + piece, slot],
            q_send.at[piece, step], q_recv.at[piece, step], (up_hist(step), cand),
        )

    for piece in range(slices):
        loop(1, nh, lambda step: q_copy(piece, step, hist).start())

    def part_copy(piece, step):
        peer = up_hist(step)
        return remote(
            part.at[piece, peer], landed.at[piece, step], part_send.at[piece, step],
            part_recv.at[piece, step], (peer, cand),
        )

    load_kv.wait()
    block = min(nh, 8)
    piece_heads = feats // head_size
    scale = 0.5 / head_size**0.5

    def attend(piece, head, base):
        cols = pl.ds(pl.multiple_of(head * head_size, head_size), head_size)
        here = pl.ds(pl.multiple_of((piece * piece_heads + head) * head_size, head_size), head_size)
        q = uq_all[slices + piece, pl.ds(base, block), :, cols].reshape(block * rows, head_size)
        k = kv[:, 0, :, here].reshape(tiles * tile_rows, head_size)
        v = kv[:, 1, :, here].reshape(tiles * tile_rows, head_size)
        weights = half_silu(times_rows(q, k) * scale).astype(BF16)
        weights = weights * mask[pl.ds(pl.multiple_of(base * rows, block * rows), block * rows), :]
        total = jnp.dot(weights, v, preferred_element_type=F32)
        part[piece, pl.ds(base, block), :, cols] = total.astype(BF16).reshape(block, rows, head_size)

    for piece in range(slices):
        loop(1, nh, lambda step: q_copy(piece, step, down_hist(step)).wait())

        def work(index, carry):
            attend(piece, lax.rem(index, piece_heads), (index // piece_heads) * block)
            return carry

        lax.fori_loop(0, piece_heads * (nh // block), work, 0)
        loop(1, nh, lambda step: part_copy(piece, step).start())

    def wf_copy(step):
        slot = down_cand(2 * step)
        return remote(wout.at[slot], wout.at[slot], wf_send.at[step], wf_recv.at[step], (hist, mate))

    def forward(step):
        w_copy(step).wait()
        wf_copy(step).start()

    loop(1, chips, forward)

    for piece in range(slices):
        loop(1, nh, lambda step: part_copy(piece, step).wait())
    attn = []
    for piece in range(slices):
        total = part[piece, hist].astype(F32)
        if nh <= 8:
            for step in range(1, nh):
                total = total + landed[piece, step].astype(F32)
        else:
            total = lax.fori_loop(
                1, nh, lambda step, acc: acc + landed[piece, step].astype(F32), total
            )
        attn.append(total)
    attn = jnp.concatenate(attn, axis=1)
    center = jnp.mean(attn, axis=1, keepdims=True)
    spread = jnp.mean((attn - center) ** 2, axis=1, keepdims=True)
    normed = (attn - center) / jnp.sqrt(spread + 1e-05)
    u = jnp.concatenate([uq_all[piece, hist] for piece in range(slices)], axis=1)
    y = (normed * u.astype(F32)).astype(BF16)

    own_w.wait()
    load_wout.wait()
    loop(1, chips, lambda step: wf_copy(step).wait())
    projected = times_rows(y, wout[...].reshape(width, width))
    out_ref[0] = (emb[0].astype(F32) + projected).astype(BF16)


def solution(mesh):
    nh, nc = mesh.shape["hist"], mesh.shape["cand"]

    def per_device(cand_emb, cand_user, kv_cache, tile_user, tile_len, w_uq, w_out):
        rows, width = cand_emb.shape[1:]
        tiles, _, tile_rows, _ = kv_cache.shape[1:]
        feats, outs = w_uq.shape[0], w_out.shape[0]
        slices = nc // 2
        dma = pltpu.SemaphoreType.DMA
        hbm = pl.BlockSpec(memory_space=pl.ANY)
        vmem = pl.BlockSpec(memory_space=pltpu.VMEM)
        smem = pl.BlockSpec(memory_space=pltpu.SMEM)
        return pl.pallas_call(
            functools.partial(kernel, nh, nc),
            out_shape=jax.ShapeDtypeStruct(cand_emb.shape, BF16),
            in_specs=[hbm, vmem, hbm, smem, smem, hbm, hbm],
            out_specs=vmem,
            scratch_shapes=[
                pltpu.VMEM((nc, rows, width), BF16),
                pltpu.VMEM((tiles, 2, tile_rows, width), BF16),
                pltpu.VMEM((feats, width), BF16),
                pltpu.VMEM((nc, outs, width), BF16),
                pltpu.VMEM((nc, rows, feats), BF16),
                pltpu.VMEM((nc, nh, rows, feats), BF16),
                pltpu.VMEM((nh * rows, tiles * tile_rows), BF16),
                pltpu.VMEM((slices, nh, rows, feats), BF16),
                pltpu.VMEM((slices, nh, rows, feats), BF16),
                dma((4,)),
                dma((nc,)), dma((nc,)),
                dma((nc,)), dma((nc,)),
                dma((slices, nh)), dma((slices, nh)),
                dma((slices, nh)), dma((slices, nh)),
                dma((nc // 2,)), dma((nc // 2,)),
                dma((nc // 2,)), dma((nc // 2,)),
            ],
            compiler_params=pltpu.CompilerParams(collective_id=0, has_side_effects=True),
        )(cand_emb, cand_user, kv_cache, tile_user, tile_len, w_uq, w_out)

    in_specs = (
        P("cand", "hist", None),
        P("cand", None),
        P("cand", "hist", None, None, None),
        P("cand", "hist"),
        P("cand", "hist"),
        P("cand", None),
        P("cand", None),
    )
    return jax.shard_map(
        per_device, mesh=mesh, in_specs=in_specs, out_specs=P("cand", "hist", None), check_vma=False
    )
```

time: 200 us -> 44.3 us (0.22)
  waiting for transfers between devices: 102 us -> 0 us
  Pallas kernels: 0 us -> 42.6 us
  blocking collectives: 31.4 us -> 0 us
  matrix products: 26.6 us -> 0 us
  other arithmetic: 13.7 us -> 0 us
  between operations: 13.3 us -> 0.01 us
  local copies, waits for them, and re-layouts: 12.6 us -> 1.47 us
    reduce_scatter x1 -> x0, waiting for transfers between devices: 63.6 us -> none  [per_device(): lax.psum_scatter(total.reshape(lax.axis_size('hist') * count, width), 'hi...]
    pallas_call x0 -> x1, Pallas kernels: none -> 42.6 us  [per_device(): pl.pallas_call(functools.partial(kernel, nh, nc), out_shape=jax.ShapeDtyp...]
    all_gather x2 -> x0, waiting for transfers between devices: 36.8 us -> none  [the longest x1 21 us: per_device(): lax.all_gather(w_out, 'cand', axis=0, tiled=True)]
    all_gather x1 -> x0, blocking collectives: 31.4 us -> none  [per_device(): all_queries = lax.all_gather(queries, 'hist', axis=0, tiled=True)]
    dot_general x10 -> x0, matrix products: 26.6 us -> none  [the longest x8 20 us: per_device(): jnp.einsum('hqk,khd->qhd', weights, values, preferred_element_type=jnp.fl...]
    unnamed x9 -> x1, local copies, waits for them, and re-layouts: 6.49 us -> 1.47 us
    lt x8 -> x0, other arithmetic: 4.92 us -> none  [per_device(): row_ids[None, :] < lengths[tile]]
    eq x1 -> x0, other arithmetic: 4.91 us -> none  [per_device(): group_users[:, None] == owners[tile]]
  transfers between devices with their start and end apart: 3 -> 0, of which waited for: 3 -> 0; matrix products, arithmetic and copies ran while one was open for 13% -> 0% of each run, Pallas kernels for 0% -> 0%
where the time goes in v1:
time: 44.3 us; the launch traced here: 44.1 us
  Pallas kernels  42.6 us (96%)
  local copies, waits for them, and re-layouts  1.47 us (3%)
    pallas_call x1, Pallas kernels, per_device(): pl.pallas_call(functools.partial(kernel, nh, nc), out_shape=jax.ShapeDtyp...  42.6 us
    unnamed x1, local copies, waits for them, and re-layouts  1.47 us

profile of v1, /device:TPU:0, one launch (start us, length us, event | category | flops | bytes accessed | tf_op | source)
XLA Modules:
  0.0 44.1 jit_solution(1831261147665139982)
XLA Ops:
  0.0 42.6 %shard_map.73 = bf16[1,32,1024]{2,1,0:T(8,128)(2,1)} custom-call(bf16[1,32,1024]{2,1,0:T(8,128)(2,1)} %emb_hbm.1, s32[1,256]{1,0:T(1,128)} %user_ref.1, bf16[1,8,2,128,1024]{4,3,2,1,0:T(8,128)(2,1)} %kv_hbm.1, s32[1,8]{1,0:T(1,128)} %owner_ref.1, s32[1,8]{1,0:T(1,128)} %len_ref.1, bf16[512,1024]{1,0:T(8,128)(2,1)} %wuq_hbm.1, bf16[256,1024]{1,0:T(8,128)(2,1)} %wout_hbm.1), custom_call_target="tpu_custom_call" | custom-call | tf_op jit(solution)/shard_map/pallas_call | solution.py:225
  42.6 1.5 %copy.9 = bf16[1,32,1024]{2,1,0:T(8,128)(2,1)} copy(bf16[1,32,1024]{2,1,0:T(8,128)(2,1)} %shard_map.73) | data formatting | bytes 131072

commit v2 on v1

v2 whole, which is shorter than its diff:
```python
import functools

import jax
import jax.numpy as jnp
from jax import lax
from jax.experimental import pallas as pl
from jax.experimental.pallas import tpu as pltpu
from jax.sharding import PartitionSpec as P

HEADS = 8
BF16 = jnp.bfloat16
F32 = jnp.float32


def times_rows(left, slab):
    return lax.dot_general(left, slab, (((1,), (1,)), ((), ())), preferred_element_type=F32)


def half_silu(half):
    return half + half * jnp.tanh(half)


def loop(low, high, body):
    if high - low <= 8:
        for step in range(low, high):
            body(step)
    else:
        lax.fori_loop(low, high, lambda step, carry: (body(step), carry)[1], 0)


def kernel(
    nx, nz, nc, emb_hbm, user_ref, kv_hbm, owner_ref, len_ref, wuq_hbm, wout_hbm, out_ref,
    emb, kv, wuq, wout, uq_send, uq_all, mask, part, landed,
    local_sem, emb_send, emb_recv, uq_ssem, uq_rsem, q_send, q_recv,
    x_send, x_recv, part_send, part_recv, w_send, w_recv, wf_send, wf_recv, news,
):
    nh = nx * nz
    hist = lax.axis_index("hist")
    z, x = hist // nx, lax.rem(hist, nx)
    own_slot = x * nz + z
    cand = lax.axis_index("cand")
    rows, width = emb.shape[1], emb.shape[2]
    feats = wuq.shape[0]
    slices = nc // 2
    head_size = width // HEADS
    tiles, tile_rows = kv.shape[0], kv.shape[2]
    chips = nc // 2
    mate = cand + 1 - 2 * lax.rem(cand, 2)

    def remote(src, dst, ssem, rsem, peer):
        return pltpu.make_async_remote_copy(
            src_ref=src, dst_ref=dst, send_sem=ssem, recv_sem=rsem,
            device_id=peer, device_id_type=pl.DeviceIdType.MESH,
        )

    def up_cand(step):
        return lax.rem(cand + step, nc)

    def down_cand(step):
        return lax.rem(cand + nc - step, nc)

    def along_z(step):
        return lax.rem(z + nz + step, nz)

    def along_x(step):
        return lax.rem(x + nx + step, nx)

    def signal(sem, hist_to, cand_to):
        pl.semaphore_signal(
            sem, inc=1, device_id=(hist_to, cand_to), device_id_type=pl.DeviceIdType.MESH
        )

    load_emb = pltpu.make_async_copy(emb_hbm.at[0], emb.at[0], local_sem.at[0])
    load_wuq = pltpu.make_async_copy(wuq_hbm, wuq, local_sem.at[1])
    load_kv = pltpu.make_async_copy(kv_hbm.at[0], kv, local_sem.at[2])
    load_wout = pltpu.make_async_copy(wout_hbm, wout.at[cand], local_sem.at[3])
    load_emb.start()
    load_wuq.start()
    load_wout.start()
    load_kv.start()

    barrier = pltpu.get_barrier_semaphore()

    loop(1, nc, lambda step: signal(barrier, hist, up_cand(step)))
    loop(1, nx, lambda step: signal(barrier, z * nx + along_x(step), cand))
    low, high = z > 0, z < nz - 1
    pl.when(low)(lambda: signal(barrier, hist - nx, cand))
    pl.when(high)(lambda: signal(barrier, hist + nx, cand))
    pl.semaphore_wait(
        barrier, nc - 1 + nx - 1 + low.astype(jnp.int32) + high.astype(jnp.int32)
    )

    def emb_copy(step):
        return remote(
            emb_hbm.at[0], emb.at[step], emb_send.at[step], emb_recv.at[step], (hist, up_cand(step))
        )

    loop(1, nc, lambda step: emb_copy(step).start())

    for far in range(2, nz):
        pl.when((z >= far - 1) & (z < nz - 1))(lambda: signal(news.at[0], hist + nx, cand))
        pl.when((z + far - 1 < nz) & (z > 0))(lambda: signal(news.at[1], hist - nx, cand))
        pl.when(z >= far)(lambda: pl.semaphore_wait(news.at[0], 1))
        pl.when(z + far < nz)(lambda: pl.semaphore_wait(news.at[1], 1))

    count = nh * rows
    users = jnp.broadcast_to(user_ref[...].astype(F32), (tile_rows, count)).T
    lane = lax.broadcasted_iota(jnp.int32, (count, tile_rows), 1)
    for tile in range(tiles):
        same = users == owner_ref[0, tile].astype(F32)
        valid = lane < len_ref[0, tile]
        mask[:, :, :, tile * tile_rows:(tile + 1) * tile_rows] = jnp.where(
            same & valid, 1.0, 0.0
        ).astype(BF16).reshape(nz, nx, rows, tile_rows)

    load_wuq.wait()
    load_emb.wait()
    loop(1, nc, lambda step: emb_copy(step).wait())
    uq = times_rows(emb[...].reshape(nc * rows, width), wuq[...])
    uq = half_silu(uq * 0.5).astype(BF16).reshape(nc, rows, feats)
    uq_send[...] = uq
    uq_all[cand, own_slot] = uq[0]

    def uq_copy(step, slot):
        return remote(
            uq_send.at[step], uq_all.at[slot, own_slot], uq_ssem.at[step], uq_rsem.at[step],
            (hist, down_cand(step)),
        )

    loop(1, nc, lambda step: uq_copy(step, cand).start())

    def w_copy(step):
        return remote(
            wout_hbm, wout.at[cand], w_send.at[step], w_recv.at[step], (hist, up_cand(2 * step))
        )

    loop(1, chips, lambda step: w_copy(step).start())
    own_w = remote(wout_hbm, wout.at[cand], w_send.at[0], w_recv.at[0], (hist, mate))
    own_w.start()

    def await_slice(source):
        step = lax.rem(source + nc - cand, nc)
        pl.when(step > 0)(lambda: uq_copy(step, source).wait_recv())

    def zq_copy(piece, step, from_z):
        block = uq_all.at[slices + piece, x * nz + from_z]
        return remote(
            block, block, q_send.at[piece, step], q_recv.at[piece, step],
            (along_z(step) * nx + x, cand),
        )

    def xq_copy(piece, over, step, from_x):
        block = uq_all.at[slices + piece, from_x * nz + along_z(-step)]
        sem = over * nz + step
        return remote(
            block, block, x_send.at[piece, sem], x_recv.at[piece, sem],
            (z * nx + along_x(over), cand),
        )

    def part_copy(piece, over, step):
        to_z, to_x = along_z(step), along_x(over)
        place = over * nz + step
        return remote(
            part.at[piece, to_x * nz + to_z], landed.at[piece, place],
            part_send.at[piece, place], part_recv.at[piece, place], (to_z * nx + to_x, cand),
        )

    def spread(piece, step):
        loop(1, nx, lambda over: xq_copy(piece, over, step, x).start())

    for piece in range(slices):
        await_slice(slices + piece)
        loop(1, nz, lambda step: zq_copy(piece, step, z).start())
        spread(piece, 0)

    load_kv.wait()
    piece_heads = feats // head_size
    scale = 0.5 / head_size**0.5
    keys = tiles * tile_rows

    def attend(piece, column):
        base = column * nz

        def work(head, carry):
            cols = pl.ds(pl.multiple_of(head * head_size, head_size), head_size)
            first = (piece * piece_heads + head) * head_size
            here = pl.ds(pl.multiple_of(first, head_size), head_size)
            q = uq_all[slices + piece, pl.ds(base, nz), :, cols].reshape(nz * rows, head_size)
            k = kv[:, 0, :, here].reshape(keys, head_size)
            v = kv[:, 1, :, here].reshape(keys, head_size)
            weights = half_silu(times_rows(q, k) * scale).astype(BF16)
            weights = weights * mask[:, column].reshape(nz * rows, keys)
            total = jnp.dot(weights, v, preferred_element_type=F32)
            part[piece, pl.ds(base, nz), :, cols] = total.astype(BF16).reshape(nz, rows, head_size)
            return carry

        lax.fori_loop(0, piece_heads, work, 0)

    def arrive(piece, step):
        zq_copy(piece, step, along_z(-step)).wait_recv()
        spread(piece, step)

    for piece in range(slices):
        loop(1, nz, lambda step: arrive(piece, step))
        attend(piece, x)
        loop(1, nz, lambda step: part_copy(piece, 0, step).start())
    for piece in range(slices):
        for over in range(1, nx):
            loop(0, nz, lambda step: xq_copy(piece, over, step, along_x(-over)).wait_recv())
            attend(piece, along_x(-over))
            loop(0, nz, lambda step: part_copy(piece, nx - over, step).start())

    def wf_copy(step):
        slot = down_cand(2 * step)
        return remote(wout.at[slot], wout.at[slot], wf_send.at[step], wf_recv.at[step], (hist, mate))

    def forward(step):
        w_copy(step).wait()
        wf_copy(step).start()

    loop(1, chips, forward)

    for piece in range(slices):
        loop(1, nz, lambda step: zq_copy(piece, step, z).wait_send())
        loop(nz, nh, lambda at: xq_copy(piece, at // nz, lax.rem(at, nz), x).wait_send())
        loop(1, nh, lambda at: part_copy(piece, at // nz, lax.rem(at, nz)).wait())
    loop(1, nc, lambda step: uq_copy(step, cand).wait_send())
    loop(0, slices, await_slice)
    attn = []
    for piece in range(slices):
        total = part[piece, own_slot].astype(F32)
        if nh <= 8:
            for step in range(1, nh):
                total = total + landed[piece, step].astype(F32)
        else:
            total = lax.fori_loop(
                1, nh, lambda step, acc: acc + landed[piece, step].astype(F32), total
            )
        attn.append(total)
    attn = jnp.concatenate(attn, axis=1)
    center = jnp.mean(attn, axis=1, keepdims=True)
    spread = jnp.mean((attn - center) ** 2, axis=1, keepdims=True)
    normed = (attn - center) / jnp.sqrt(spread + 1e-05)
    u = jnp.concatenate([uq_all[piece, own_slot] for piece in range(slices)], axis=1)
    y = (normed * u.astype(F32)).astype(BF16)

    own_w.wait()
    load_wout.wait()
    loop(1, chips, lambda step: wf_copy(step).wait())
    projected = times_rows(y, wout[...].reshape(width, width))
    out_ref[0] = (emb[0].astype(F32) + projected).astype(BF16)


def solution(mesh):
    nh, nc = mesh.shape["hist"], mesh.shape["cand"]
    nx = 1 << ((nh.bit_length() - 1) // 2)
    nz = nh // nx

    def per_device(cand_emb, cand_user, kv_cache, tile_user, tile_len, w_uq, w_out):
        rows, width = cand_emb.shape[1:]
        tiles, _, tile_rows, _ = kv_cache.shape[1:]
        feats, outs = w_uq.shape[0], w_out.shape[0]
        slices = nc // 2
        dma = pltpu.SemaphoreType.DMA
        hbm = pl.BlockSpec(memory_space=pl.ANY)
        vmem = pl.BlockSpec(memory_space=pltpu.VMEM)
        smem = pl.BlockSpec(memory_space=pltpu.SMEM)
        return pl.pallas_call(
            functools.partial(kernel, nx, nz, nc),
            out_shape=jax.ShapeDtypeStruct(cand_emb.shape, BF16),
            in_specs=[hbm, vmem, hbm, smem, smem, hbm, hbm],
            out_specs=vmem,
            scratch_shapes=[
                pltpu.VMEM((nc, rows, width), BF16),
                pltpu.VMEM((tiles, 2, tile_rows, width), BF16),
                pltpu.VMEM((feats, width), BF16),
                pltpu.VMEM((nc, outs, width), BF16),
                pltpu.VMEM((nc, rows, feats), BF16),
                pltpu.VMEM((nc, nh, rows, feats), BF16),
                pltpu.VMEM((nz, nx, rows, tiles * tile_rows), BF16),
                pltpu.VMEM((slices, nh, rows, feats), BF16),
                pltpu.VMEM((slices, nh, rows, feats), BF16),
                dma((4,)),
                dma((nc,)), dma((nc,)),
                dma((nc,)), dma((nc,)),
                dma((slices, nz)), dma((slices, nz)),
                dma((slices, nh)), dma((slices, nh)),
                dma((slices, nh)), dma((slices, nh)),
                dma((nc // 2,)), dma((nc // 2,)),
                dma((nc // 2,)), dma((nc // 2,)),
                pltpu.SemaphoreType.REGULAR((2,)),
            ],
            compiler_params=pltpu.CompilerParams(collective_id=0, has_side_effects=True),
        )(cand_emb, cand_user, kv_cache, tile_user, tile_len, w_uq, w_out)

    in_specs = (
        P("cand", "hist", None),
        P("cand", None),
        P("cand", "hist", None, None, None),
        P("cand", "hist"),
        P("cand", "hist"),
        P("cand", None),
        P("cand", None),
    )
    return jax.shard_map(
        per_device, mesh=mesh, in_specs=in_specs, out_specs=P("cand", "hist", None), check_vma=False
    )
```

time: 44.3 us -> 37.5 us (0.85)
  Pallas kernels: 42.6 us -> 35.9 us
    pallas_call x1, Pallas kernels: 42.6 us -> 35.9 us  [per_device(): pl.pallas_call(functools.partial(kernel, nx, nz, nc), out_shape=jax.Shape...]
where the time goes in v2:
time: 37.5 us; the launch traced here: 37.4 us
  Pallas kernels  35.9 us (96%)
  local copies, waits for them, and re-layouts  1.47 us (4%)
    pallas_call x1, Pallas kernels, per_device(): pl.pallas_call(functools.partial(kernel, nx, nz, nc), out_shape=jax.Shape...  35.9 us
    unnamed x1, local copies, waits for them, and re-layouts  1.47 us

profile of v2, /device:TPU:0, one launch (start us, length us, event | category | flops | bytes accessed | tf_op | source)
XLA Modules:
  0.0 37.4 jit_solution(9864569956595918466)
XLA Ops:
  0.0 35.9 %shard_map.73 = bf16[1,32,1024]{2,1,0:T(8,128)(2,1)} custom-call(bf16[1,32,1024]{2,1,0:T(8,128)(2,1)} %emb_hbm.1, s32[1,256]{1,0:T(1,128)} %user_ref.1, bf16[1,8,2,128,1024]{4,3,2,1,0:T(8,128)(2,1)} %kv_hbm.1, s32[1,8]{1,0:T(1,128)} %owner_ref.1, s32[1,8]{1,0:T(1,128)} %len_ref.1, bf16[512,1024]{1,0:T(8,128)(2,1)} %wuq_hbm.1, bf16[256,1024]{1,0:T(8,128)(2,1)} %wout_hbm.1), custom_call_target="tpu_custom_call" | custom-call | tf_op jit(solution)/shard_map/pallas_call | solution.py:268
  35.9 1.5 %copy.9 = bf16[1,32,1024]{2,1,0:T(8,128)(2,1)} copy(bf16[1,32,1024]{2,1,0:T(8,128)(2,1)} %shard_map.73) | data formatting | bytes 131072

commit v3 on v2

--- a/solution.py
+++ b/solution.py
@@ -29,10 +29,10 @@
 
 
 def kernel(
-    nx, nz, nc, emb_hbm, user_ref, kv_hbm, owner_ref, len_ref, wuq_hbm, wout_hbm, out_ref,
-    emb, kv, wuq, wout, uq_send, uq_all, mask, part, landed,
+    nx, nz, nc, emb_hbm, user_hbm, kv_hbm, owner_hbm, len_hbm, wuq_hbm, wout_hbm, out_ref,
+    user_ref, owner_ref, len_ref, emb, kv, wuq, wout, uq_send, uq_all, mask, part, landed,
     local_sem, emb_send, emb_recv, uq_ssem, uq_rsem, q_send, q_recv,
-    x_send, x_recv, part_send, part_recv, w_send, w_recv, wf_send, wf_recv, news,
+    x_send, x_recv, part_send, part_recv, w_send, w_recv, wf_send, wf_recv, news, far_send,
 ):
     nh = nx * nz
     hist = lax.axis_index("hist")
@@ -74,7 +74,15 @@
     load_wuq = pltpu.make_async_copy(wuq_hbm, wuq, local_sem.at[1])
     load_kv = pltpu.make_async_copy(kv_hbm.at[0], kv, local_sem.at[2])
     load_wout = pltpu.make_async_copy(wout_hbm, wout.at[cand], local_sem.at[3])
+    load_small = [
+        pltpu.make_async_copy(src, dst, local_sem.at[4 + at])
+        for at, (src, dst) in enumerate(
+            ((user_hbm, user_ref), (owner_hbm, owner_ref), (len_hbm, len_ref))
+        )
+    ]
     load_emb.start()
+    for load in load_small:
+        load.start()
     load_wuq.start()
     load_wout.start()
     load_kv.start()
@@ -97,12 +105,14 @@
 
     loop(1, nc, lambda step: emb_copy(step).start())
 
-    for far in range(2, nz):
+    for far in range(1, nz):
         pl.when((z >= far - 1) & (z < nz - 1))(lambda: signal(news.at[0], hist + nx, cand))
         pl.when((z + far - 1 < nz) & (z > 0))(lambda: signal(news.at[1], hist - nx, cand))
         pl.when(z >= far)(lambda: pl.semaphore_wait(news.at[0], 1))
         pl.when(z + far < nz)(lambda: pl.semaphore_wait(news.at[1], 1))
 
+    for load in load_small:
+        load.wait()
     count = nh * rows
     users = jnp.broadcast_to(user_ref[...].astype(F32), (tile_rows, count)).T
     lane = lax.broadcasted_iota(jnp.int32, (count, tile_rows), 1)
@@ -129,6 +139,20 @@
 
     loop(1, nc, lambda step: uq_copy(step, cand).start())
 
+    half = nz // 2
+    takes_far = cand < slices
+
+    def far_copy(step):
+        return remote(
+            uq_send.at[step], uq_all.at[slices, own_slot], far_send.at[step], q_recv.at[0, half],
+            (along_z(half) * nx + x, down_cand(step)),
+        )
+
+    def if_far(step, action):
+        pl.when((cand == slices) & (down_cand(step) < slices))(lambda: action(far_copy(step)))
+
+    loop(1, nc, lambda step: if_far(step, lambda copy: copy.start()))
+
     def w_copy(step):
         return remote(
             wout_hbm, wout.at[cand], w_send.at[step], w_recv.at[step], (hist, up_cand(2 * step))
@@ -165,12 +189,18 @@
             part_send.at[piece, place], part_recv.at[piece, place], (to_z * nx + to_x, cand),
         )
 
+    def if_near(piece, step, action):
+        if piece > 0:
+            action(zq_copy(piece, step, z))
+        else:
+            pl.when(~takes_far | (step != half))(lambda: action(zq_copy(piece, step, z)))
+
     def spread(piece, step):
         loop(1, nx, lambda over: xq_copy(piece, over, step, x).start())
 
     for piece in range(slices):
         await_slice(slices + piece)
-        loop(1, nz, lambda step: zq_copy(piece, step, z).start())
+        loop(1, nz, lambda step: if_near(piece, step, lambda copy: copy.start()))
         spread(piece, 0)
 
     load_kv.wait()
@@ -221,10 +251,11 @@
     loop(1, chips, forward)
 
     for piece in range(slices):
-        loop(1, nz, lambda step: zq_copy(piece, step, z).wait_send())
+        loop(1, nz, lambda step: if_near(piece, step, lambda copy: copy.wait_send()))
         loop(nz, nh, lambda at: xq_copy(piece, at // nz, lax.rem(at, nz), x).wait_send())
         loop(1, nh, lambda at: part_copy(piece, at // nz, lax.rem(at, nz)).wait())
     loop(1, nc, lambda step: uq_copy(step, cand).wait_send())
+    loop(1, nc, lambda step: if_far(step, lambda copy: copy.wait_send()))
     loop(0, slices, await_slice)
     attn = []
     for piece in range(slices):
@@ -264,13 +295,15 @@
         dma = pltpu.SemaphoreType.DMA
         hbm = pl.BlockSpec(memory_space=pl.ANY)
         vmem = pl.BlockSpec(memory_space=pltpu.VMEM)
-        smem = pl.BlockSpec(memory_space=pltpu.SMEM)
         return pl.pallas_call(
             functools.partial(kernel, nx, nz, nc),
             out_shape=jax.ShapeDtypeStruct(cand_emb.shape, BF16),
-            in_specs=[hbm, vmem, hbm, smem, smem, hbm, hbm],
+            in_specs=[hbm] * 7,
             out_specs=vmem,
             scratch_shapes=[
+                pltpu.VMEM(cand_user.shape, jnp.int32),
+                pltpu.SMEM(tile_user.shape, jnp.int32),
+                pltpu.SMEM(tile_len.shape, jnp.int32),
                 pltpu.VMEM((nc, rows, width), BF16),
                 pltpu.VMEM((tiles, 2, tile_rows, width), BF16),
                 pltpu.VMEM((feats, width), BF16),
@@ -280,7 +313,7 @@
                 pltpu.VMEM((nz, nx, rows, tiles * tile_rows), BF16),
                 pltpu.VMEM((slices, nh, rows, feats), BF16),
                 pltpu.VMEM((slices, nh, rows, feats), BF16),
-                dma((4,)),
+                dma((7,)),
                 dma((nc,)), dma((nc,)),
                 dma((nc,)), dma((nc,)),
                 dma((slices, nz)), dma((slices, nz)),
@@ -289,6 +322,7 @@
                 dma((nc // 2,)), dma((nc // 2,)),
                 dma((nc // 2,)), dma((nc // 2,)),
                 pltpu.SemaphoreType.REGULAR((2,)),
+                dma((nc,)),
             ],
             compiler_params=pltpu.CompilerParams(collective_id=0, has_side_effects=True),
         )(cand_emb, cand_user, kv_cache, tile_user, tile_len, w_uq, w_out)

time: 37.5 us -> 36 us (0.960)
  Pallas kernels: 35.9 us -> 34.4 us
    pallas_call x1, Pallas kernels: 35.9 us -> 34.4 us  [per_device(): pl.pallas_call(functools.partial(kernel, nx, nz, nc), out_shape=jax.Shape...]
where the time goes in v3:
time: 36 us; the launch traced here: 35.9 us
  Pallas kernels  34.4 us (96%)
  local copies, waits for them, and re-layouts  1.47 us (4%)
    pallas_call x1, Pallas kernels, per_device(): pl.pallas_call(functools.partial(kernel, nx, nz, nc), out_shape=jax.Shape...  34.4 us
    unnamed x1, local copies, waits for them, and re-layouts  1.47 us

profile of v3, /device:TPU:0, one launch (start us, length us, event | category | flops | bytes accessed | tf_op | source)
XLA Modules:
  0.0 35.9 jit_solution(4451934247261742102)
XLA Ops:
  0.0 34.4 %shard_map.73 = bf16[1,32,1024]{2,1,0:T(8,128)(2,1)} custom-call(bf16[1,32,1024]{2,1,0:T(8,128)(2,1)} %emb_hbm.1, s32[1,256]{1,0:T(1,128)} %user_hbm.1, bf16[1,8,2,128,1024]{4,3,2,1,0:T(8,128)(2,1)} %kv_hbm.1, s32[1,8]{1,0:T(1,128)} %owner_hbm.1, s32[1,8]{1,0:T(1,128)} %len_hbm.1, bf16[512,1024]{1,0:T(8,128)(2,1)} %wuq_hbm.1, bf16[256,1024]{1,0:T(8,128)(2,1)} %wout_hbm.1), custom_call_target="tpu_custom_call" | custom-call | tf_op jit(solution)/shard_map/pallas_call | solution.py:298
  34.4 1.5 %copy.9 = bf16[1,32,1024]{2,1,0:T(8,128)(2,1)} copy(bf16[1,32,1024]{2,1,0:T(8,128)(2,1)} %shard_map.73) | data formatting | bytes 131072

commit v4 on v3

--- a/solution.py
+++ b/solution.py
@@ -250,15 +250,10 @@
 
     loop(1, chips, forward)
 
-    for piece in range(slices):
-        loop(1, nz, lambda step: if_near(piece, step, lambda copy: copy.wait_send()))
-        loop(nz, nh, lambda at: xq_copy(piece, at // nz, lax.rem(at, nz), x).wait_send())
-        loop(1, nh, lambda at: part_copy(piece, at // nz, lax.rem(at, nz)).wait())
-    loop(1, nc, lambda step: uq_copy(step, cand).wait_send())
-    loop(1, nc, lambda step: if_far(step, lambda copy: copy.wait_send()))
     loop(0, slices, await_slice)
     attn = []
     for piece in range(slices):
+        loop(1, nh, lambda at: part_copy(piece, at // nz, lax.rem(at, nz)).wait_recv())
         total = part[piece, own_slot].astype(F32)
         if nh <= 8:
             for step in range(1, nh):
@@ -280,6 +275,12 @@
     loop(1, chips, lambda step: wf_copy(step).wait())
     projected = times_rows(y, wout[...].reshape(width, width))
     out_ref[0] = (emb[0].astype(F32) + projected).astype(BF16)
+    for piece in range(slices):
+        loop(1, nz, lambda step: if_near(piece, step, lambda copy: copy.wait_send()))
+        loop(nz, nh, lambda at: xq_copy(piece, at // nz, lax.rem(at, nz), x).wait_send())
+        loop(1, nh, lambda at: part_copy(piece, at // nz, lax.rem(at, nz)).wait_send())
+    loop(1, nc, lambda step: uq_copy(step, cand).wait_send())
+    loop(1, nc, lambda step: if_far(step, lambda copy: copy.wait_send()))
 
 
 def solution(mesh):

time: 36 us -> 36 us (level)
  no operation moved by 1% of the time
where the time goes in v4:
time: 36 us; the launch traced here: 35.9 us
  Pallas kernels  34.4 us (96%)
  local copies, waits for them, and re-layouts  1.47 us (4%)
    pallas_call x1, Pallas kernels, per_device(): pl.pallas_call(functools.partial(kernel, nx, nz, nc), out_shape=jax.Shape...  34.4 us
    unnamed x1, local copies, waits for them, and re-layouts  1.47 us

profile of v4, /device:TPU:0, one launch (start us, length us, event | category | flops | bytes accessed | tf_op | source)
XLA Modules:
  0.0 35.9 jit_solution(6742129414391288931)
XLA Ops:
  0.0 34.4 %shard_map.73 = bf16[1,32,1024]{2,1,0:T(8,128)(2,1)} custom-call(bf16[1,32,1024]{2,1,0:T(8,128)(2,1)} %emb_hbm.1, s32[1,256]{1,0:T(1,128)} %user_hbm.1, bf16[1,8,2,128,1024]{4,3,2,1,0:T(8,128)(2,1)} %kv_hbm.1, s32[1,8]{1,0:T(1,128)} %owner_hbm.1, s32[1,8]{1,0:T(1,128)} %len_hbm.1, bf16[512,1024]{1,0:T(8,128)(2,1)} %wuq_hbm.1, bf16[256,1024]{1,0:T(8,128)(2,1)} %wout_hbm.1), custom_call_target="tpu_custom_call" | custom-call | tf_op jit(solution)/shard_map/pallas_call | solution.py:299
  34.4 1.5 %copy.9 = bf16[1,32,1024]{2,1,0:T(8,128)(2,1)} copy(bf16[1,32,1024]{2,1,0:T(8,128)(2,1)} %shard_map.73) | data formatting | bytes 131072
